TPU v7x, 128 devices: a whole 4x4x4 slice. The times are simulated.
128 devices in a mesh: gx: 4 (over y), gy: 4 (over x_lo, core), gz: 8 (over z, x_hi).
Axes of the slice: x: 4 (x_hi: 2, x_lo: 2; x = x_hi * 2 + x_lo), y: 4, z: 4, core: 2. Of those that a mesh axis runs over, the one named last changes fastest.
Arguments:
- forcing: float32 [128, 128, 1024], P('gx', 'gy', 'gz'), may hold values from -6 to 6
- kappa_base: float32 [128, 128, 1024], P('gx', 'gy', 'gz'), may hold values from 0.5 to 2
- labels: int32 [128, 128, 1024], P('gx', 'gy', 'gz'), may hold values from 0 to 3
- contrast: float32 [4], replicated, may hold values from 1 to 100
- channel_weight: float32 [4], replicated, may hold values from 0.25 to 2
- coarse_coef: float32 [4, 4, 8, 64, 8], P('gx', 'gy', 'gz'), may hold values from -6 to 6
- source_link: int32 [4, 4, 8, 40, 4], P('gx', 'gy', 'gz'), may hold values from 0 to 63, as said below
- offsets: int32 [4, 4, 8, 40, 3], P('gx', 'gy', 'gz'), may hold values from 0 to 120, as said below
- live_pieces: int32 [4, 4, 8], P('gx', 'gy', 'gz'), may hold values from 5 to 40, as said below
- resident_bases: float32 [4, 4, 8, 40, 8, 4096], P('gx', 'gy', 'gz'), may hold values from -5 to 5
Outputs:
- update: float32 [128, 128, 1024], P('gx', 'gy', 'gz')
- new_basis: float32 [4, 4, 8, 40, 2, 4096], P('gx', 'gy', 'gz')
Inputs may be any that keep to these rules, and one draw needn't show every extreme that they name: `source_link`: each of the three brick offsets of a slot, minus one, leads to a brick inside the mesh; a coefficient slot may be named by several pieces. `offsets`: every piece lies inside its brick's padded frame of (40) x (40) x (136) cells. `live_pieces`: some brick has all 40 slots live in every draw.
All inputs are finite; a program needn't handle non-finite values.
Results may differ from a plain program's by a relative error of at most 0.0003.
Values sent between devices are 32-bit elements; how exact they have to be, the bound alone decides.
A program may use at most 128 MiB of HBM per device.

v0:
```python
import jax
import jax.numpy as jnp
from jax import lax
from jax.experimental import pallas as pl
from jax.experimental.pallas import tpu as pltpu
from jax.sharding import PartitionSpec as P

ND = 64
PIECE=16; NB=8; NP=40; SWEEPS=20
OMEGA = 2.0/3.0
PAIR = 8
FEW = 8
VM = pl.BlockSpec(memory_space=pltpu.VMEM)
SM = pl.BlockSpec(memory_space=pltpu.SMEM)
ANY = pl.BlockSpec(memory_space=pltpu.HBM)

def corner(off, p):
    ox = jnp.clip(off[0, 0, p], 0, 24)
    oy = jnp.clip(off[1, 0, p], 0, 24)
    oz = jnp.clip(off[2, 0, p], 0, 120)
    tile = (oz > 112).astype(jnp.int32)
    return ox, oy, tile, oz - 8 * tile

def rot(v, shift, axis=1):
    return pltpu.roll(v, shift, axis)

def lanes_sub():
    return lax.broadcasted_iota(jnp.int32, (8, 128), 1), lax.broadcasted_iota(jnp.int32, (8, 128), 0)

MESH = pl.DeviceIdType.MESH
SIZE = {"gx": 4, "gy": 4, "gz": 8}


def ring(axis, step):
    n = SIZE[axis]
    return lax.rem(lax.axis_index(axis) + (step + n), n)


def greet(pairs):
    barrier = pltpu.get_barrier_semaphore()
    for axis, step in pairs:
        pl.semaphore_signal(barrier, inc=1, device_id={axis: ring(axis, step)}, device_id_type=MESH)
    pl.semaphore_wait(barrier, len(pairs))


def remote(src, dst, send, recv, i, axis, step):
    copy = pltpu.make_async_remote_copy(
        src_ref=src, dst_ref=dst, send_sem=send.at[i], recv_sem=recv.at[i],
        device_id={axis: ring(axis, step)}, device_id_type=MESH,
    )
    copy.start()
    return copy


def edges(axis):
    i = lax.axis_index(axis)
    return (jnp.where(i > 0, 1.0, 0.0), jnp.where(i < SIZE[axis] - 1, 1.0, 0.0))


def group_row(g, pos):
    return 8 * g - 4 + pos


def share_kernel(coef, forcing, base, labels, con, chw, basis, gat, E, G, yk, held, bsem, tile, col, zs, zr, yr, xs, xr, send, recv):
    ix, iy, iz = lax.axis_index("gx"), lax.axis_index("gy"), lax.axis_index("gz")
    lane, sub = lanes_sub()
    tile[...] = jnp.zeros_like(tile)
    tile[0:8, 0:64] = coef[...]
    fetch = pltpu.make_async_copy(basis, held, bsem)
    fetch.start()
    greet([("gz", s) for s in range(1, 8)] + [("gy", s) for s in range(1, 4)] + [("gx", s) for s in range(1, 4)])
    g1 = [remote(tile, col.at[iz], send, recv, s - 1, "gz", s) for s in range(1, 8)]
    col[iz] = tile[...]

    def fill(x, c):
        for yo in range(4):
            rows = pl.ds(pl.multiple_of(x * 32 + 8 * yo, 8), 8)
            lab = labels[rows, :]
            kappa = jnp.zeros((8, 128), jnp.float32)
            weight = jnp.zeros((8, 128), jnp.float32)
            for ch in range(4):
                kappa = jnp.where(lab == ch, con[ch], kappa)
                weight = jnp.where(lab == ch, chw[ch], weight)
            for f, v in enumerate((forcing[rows, :], base[rows, :] * kappa, weight)):
                E[pl.ds((48 * f + 8 + 8 * yo) * 48 + 8 + x, 8, stride=48), :] = v
                @pl.when(x >= 27)
                def _():
                    xs[0, f, x - 27, pl.ds(8 * yo, 8), :] = v
                @pl.when(x < 5)
                def _():
                    xs[1, f, x, pl.ds(8 * yo, 8), :] = v
        return c

    lax.fori_loop(0, 32, fill, 0, unroll=2)
    xm = [remote(xs.at[0], xr.at[0], send, recv, 7, "gx", 1), remote(xs.at[1], xr.at[1], send, recv, 8, "gx", -1)]

    def stagey(n, c):
        f, k = n // 5, lax.rem(n, 5)
        zs_hi = (48 * f + 35 + k) * 48 + 8
        zs_lo = (48 * f + 8 + k) * 48 + 8
        yr[0, f, k] = E[pl.ds(pl.multiple_of(zs_hi, 8), 32), :]
        yr[1, f, k] = E[pl.ds(pl.multiple_of(zs_lo, 8), 32), :]
        return c

    lax.fori_loop(0, 15, stagey, 0)
    yc = [remote(yr.at[0], yr.at[2], send, recv, 9, "gy", 1), remote(yr.at[1], yr.at[3], send, recv, 10, "gy", -1)]
    lane8 = lane // 8

    def packz(n, c):
        f, q, xo = n // 8, lax.rem(n // 4, 2), lax.rem(n, 4)
        top, bottom = None, None
        for i in range(16):
            v = E[pl.ds(pl.multiple_of((48 * f + 8 + 16 * q + i) * 48 + 8 + 8 * xo, 8), 8), :]
            hi = rot(v, (8 * i + 8) % 128)
            lo = rot(v, (8 * i) % 128) if i else v
            top = hi if i == 0 else jnp.where(lane8 == i, hi, top)
            bottom = lo if i == 0 else jnp.where(lane8 == i, lo, bottom)
        zs[0, f, q, pl.ds(pl.multiple_of(8 * xo, 8), 8), :] = top
        zs[1, f, q, pl.ds(pl.multiple_of(8 * xo, 8), 8), :] = bottom
        return c

    lax.fori_loop(0, 24, packz, 0)
    zc = [remote(zs.at[0], zr.at[0], send, recv, 11, "gz", 1), remote(zs.at[1], zr.at[1], send, recv, 12, "gz", -1)]
    for c in g1:
        c.wait()
    mine = ix * 4 + iy
    for h in range(4):
        gat[mine, h] = jnp.where(lane < 64, col[2 * h], rot(col[2 * h + 1], 64))
    g2 = [remote(gat.at[mine], gat.at[mine], send, recv, 12 + s, "gy", s) for s in range(1, 4)]

    my, py = edges("gy")
    mx, px = edges("gx")
    mz, pz = edges("gz")
    for c in yc:
        c.wait()
    for c in g2:
        c.wait()
    plane = pl.ds(ix * 4, 4)
    g3 = [remote(gat.at[plane], gat.at[plane], send, recv, 15 + s, "gx", s) for s in range(1, 4)]

    def addy(n, c):
        f, k = n // 5, lax.rem(n, 5)
        for d, y0, m in ((0, 3, my), (1, 40, py)):
            v = yr[2 + d, f, k] * m
            E[pl.ds(pl.multiple_of((48 * f + y0 + k) * 48 + 8, 8), 32), :] = v
            yk[0, d, f, k] = v[24:32, :]
            yk[1, d, f, k] = v[0:8, :]
        return c

    lax.fori_loop(0, 15, addy, 0)
    for c in zc:
        c.wait()
    lane16 = lane // 16
    low = lax.rem(lane, 16) < 8

    def windows(n, c):
        f, xo = n // 4, lax.rem(n, 4)
        rows = pl.ds(pl.multiple_of(8 * xo, 8), 8)
        src = [[zr[d, f, q, rows, :] * m for q in range(2)] for d, m in ((0, mz), (1, pz))]
        for g in range(1, 6):
            acc = jnp.zeros((8, 128), jnp.float32)
            for pos in range(8):
                y = group_row(g, pos) - 8
                if y < 0 or y > 31:
                    continue
                a = rot(src[0][y // 16], (16 * pos - 8 * (y % 16)) % 128)
                b = rot(src[1][y // 16], (16 * pos + 8 - 8 * (y % 16)) % 128)
                acc = jnp.where(lane16 == pos, jnp.where(low, a, b), acc)
            G[f, g, pl.ds(pl.multiple_of(8 + 8 * xo, 8), 8), :] = acc
        return c

    lax.fori_loop(0, 12, windows, 0)
    for c in xm:
        c.wait()

    def addx(n, c):
        f, k = n // 5, lax.rem(n, 5)
        for yo in range(4):
            E[pl.ds((48 * f + 8 + 8 * yo) * 48 + 3 + k, 8, stride=48), :] = xr[0, f, k, pl.ds(8 * yo, 8), :] * mx
            E[pl.ds((48 * f + 8 + 8 * yo) * 48 + 40 + k, 8, stride=48), :] = xr[1, f, k, pl.ds(8 * yo, 8), :] * px
        return c

    lax.fori_loop(0, 15, addx, 0)
    for c in g3:
        c.wait()
    fetch.wait()


HALO = [("gy", 1), ("gy", -1), ("gx", 1), ("gx", -1), ("gz", 1), ("gz", -1)]


def split_rows(T, ey, rows):
    lane, _ = lanes_sub()
    t0 = rot(T[0, ey, rows, :], 124)
    t1 = rot(T[1, ey, rows, :], 4)
    a = jnp.where(lane < 124, t0, 0.0) + jnp.where(lane >= 4, t1, 0.0)
    m = jnp.where(lane >= 124, t0, jnp.where(lane < 4, t1, 0.0))
    return a, m


def merge_kernel(T, G0, yk, E, W, G, xk, yg, xg, kr, zs, zr, yr, yw, xs, xr, xws, xwr, send, recv):
    greet(HALO)
    cc = [remote(yk.at[0], kr.at[0], send, recv, 10, "gx", 1), remote(yk.at[1], kr.at[1], send, recv, 11, "gx", -1)]
    gc = [remote(G0.at[:, pl.ds(4, 2), pl.ds(8, 32)], yg.at[0], send, recv, 12, "gy", 1),
          remote(G0.at[:, pl.ds(1, 2), pl.ds(8, 32)], yg.at[1], send, recv, 13, "gy", -1)]
    lane, sub = lanes_sub()
    lane16 = lane // 16
    low = lax.rem(lane, 16) < 8
    E[3] = jnp.zeros((48, 128), jnp.float32)
    E[44] = jnp.zeros((48, 128), jnp.float32)

    def build(n, c):
        g, xo = 1 + n // 6, lax.rem(n, 6)
        rows = pl.ds(pl.multiple_of(8 * xo, 8), 8)
        nxt, prv, own = None, None, None
        for pos in range(8):
            ey = 8 * g - 4 + pos
            a, m = split_rows(T, ey, rows)
            E[ey, rows, :] = a
            ra = rot(a, (16 * pos + 8) % 128)
            rm = rot(m, (16 * pos + 8) % 128)
            s0, s1 = jnp.where(low, ra, rm), jnp.where(low, rm, ra)
            if pos == 0:
                nxt, prv, own = s0, s1, rm
            else:
                hit = lane16 == pos
                nxt, prv, own = jnp.where(hit, s0, nxt), jnp.where(hit, s1, prv), jnp.where(hit, rm, own)
        zs[0, g - 1, rows, :] = nxt
        zs[1, g - 1, rows, :] = prv
        W[0, g, rows, :] = own
        return c

    lax.fori_loop(0, 30, build, 0)
    zc = [remote(zs.at[0], zr.at[0], send, recv, 2, "gz", 1), remote(zs.at[1], zr.at[1], send, recv, 3, "gz", -1)]
    yc = [remote(E.at[pl.ds(35, 9)], yr.at[0], send, recv, 0, "gy", 1), remote(E.at[pl.ds(4, 9)], yr.at[1], send, recv, 1, "gy", -1)]
    my, py = edges("gy")
    mz, pz = edges("gz")
    mx, px = edges("gx")
    for c in gc:
        c.wait()
    inner = pl.ds(8, 32)
    for f in range(3):
        G[f, 0, inner, :] = yg[0, f, 0] * my
        G[f, 1, inner, :] = G0[f, 1, inner, :] + yg[0, f, 1] * my
        for g in (2, 3, 4):
            G[f, g, inner, :] = G0[f, g, inner, :]
        G[f, 5, inner, :] = G0[f, 5, inner, :] + yg[1, f, 0] * py
        G[f, 6, inner, :] = yg[1, f, 1] * py
    hc = [remote(G.at[:, :, pl.ds(32, 8)], xg.at[0], send, recv, 14, "gx", 1), remote(G.at[:, :, pl.ds(8, 8)], xg.at[1], send, recv, 15, "gx", -1)]
    for c in yc:
        c.wait()
    def addy(k, c):
        E[3 + k] += yr[0, k] * my
        E[36 + k] += yr[1, k] * py
        return c
    lax.fori_loop(0, 9, addy, 0)
    def stage(y, c):
        xs[0, pl.ds(y * 9, 9), :] = E[3 + y, pl.ds(35, 9), :]
        xs[1, pl.ds(y * 9, 9), :] = E[3 + y, pl.ds(4, 9), :]
        return c
    lax.fori_loop(0, 42, stage, 0, unroll=6)
    xc = [remote(xs.at[0], xr.at[0], send, recv, 4, "gx", 1), remote(xs.at[1], xr.at[1], send, recv, 5, "gx", -1)]
    for c in zc:
        c.wait()
    def windows(n, c):
        g, xo = n // 6, lax.rem(n, 6)
        rows = pl.ds(pl.multiple_of(8 * xo, 8), 8)
        x, y = zr[0, g, rows, :] * mz, zr[1, g, rows, :] * pz
        W[0, g + 1, rows, :] += jnp.where(low, x, y)
        W[1, g + 1, rows, :] = jnp.where(low, y, x)
        return c
    lax.fori_loop(0, 30, windows, 0)
    wc = [remote(W.at[:, pl.ds(4, 2)], yw.at[0], send, recv, 6, "gy", 1), remote(W.at[:, pl.ds(1, 2)], yw.at[1], send, recv, 7, "gy", -1)]
    for c in wc:
        c.wait()
    for w in range(2):
        for k in range(2):
            a, b = yw[0, w, k] * my, yw[1, w, k] * py
            W[w, k] = a if k == 0 else W[w, k] + a
            W[w, 5 + k] = b if k == 1 else W[w, 5 + k] + b
    def stagew(n, c):
        w, g = n // 7, lax.rem(n, 7)
        xws[0, pl.ds(n * 9, 9), :] = W[w, g, pl.ds(35, 9), :]
        xws[1, pl.ds(n * 9, 9), :] = W[w, g, pl.ds(4, 9), :]
        return c
    lax.fori_loop(0, 14, stagew, 0, unroll=7)
    vc = [remote(xws.at[0], xwr.at[0], send, recv, 8, "gx", 1), remote(xws.at[1], xwr.at[1], send, recv, 9, "gx", -1)]
    for c in cc + hc:
        c.wait()
    for d in range(2):
        for f in range(3):
            for k in range(5):
                xk[0, d, f, k] = kr[0, d, f, k] * mx
                xk[1, d, f, k] = kr[1, d, f, k] * px
    for f in range(3):
        for g in range(7):
            G[f, g, pl.ds(0, 8), :] = xg[0, f, g] * mx
            G[f, g, pl.ds(40, 8), :] = xg[1, f, g] * px
    for c in xc:
        c.wait()
    def unstage(y, c):
        E[3 + y, pl.ds(3, 9), :] += xr[0, pl.ds(y * 9, 9), :] * mx
        E[3 + y, pl.ds(36, 9), :] += xr[1, pl.ds(y * 9, 9), :] * px
        return c
    lax.fori_loop(0, 42, unstage, 0, unroll=6)
    for c in vc:
        c.wait()
    def unstagew(n, c):
        w, g = n // 7, lax.rem(n, 7)
        W[w, g, pl.ds(3, 9), :] += xwr[0, pl.ds(n * 9, 9), :] * mx
        W[w, g, pl.ds(36, 9), :] += xwr[1, pl.ds(n * 9, 9), :] * px
        return c
    lax.fori_loop(0, 14, unstagew, 0, unroll=7)


def fold_kernel(T, C, upd, E, zs, zr, yr, xs, xr, send, recv):
    greet(HALO)
    lane, sub = lanes_sub()
    lane8 = lane // 8

    def build(n, c):
        q, xo = n // 6, lax.rem(n, 6)
        rows = pl.ds(pl.multiple_of(8 * xo, 8), 8)
        nxt, prv = None, None
        for i in range(16):
            ey = 4 + 16 * q + i
            a, m = split_rows(T, ey, rows)
            E[ey, rows, :] = a
            hi = rot(m, (8 * i) % 128) if i else m
            lo = rot(m, (8 * i + 8) % 128)
            nxt = hi if i == 0 else jnp.where(lane8 == i, hi, nxt)
            prv = lo if i == 0 else jnp.where(lane8 == i, lo, prv)
        zs[0, q, rows, :] = nxt
        zs[1, q, rows, :] = prv
        return c

    lax.fori_loop(0, 18, build, 0)
    zc = [remote(zs.at[0], zr.at[0], send, recv, 0, "gz", 1), remote(zs.at[1], zr.at[1], send, recv, 1, "gz", -1)]
    my, py = edges("gy")
    mz, pz = edges("gz")
    mx, px = edges("gx")
    for c in zc:
        c.wait()
    def addz(n, c):
        q, xo = n // 6, lax.rem(n, 6)
        rows = pl.ds(pl.multiple_of(8 * xo, 8), 8)
        x, y = zr[0, q, rows, :] * mz, zr[1, q, rows, :] * pz
        for i in range(16):
            a = rot(x, (128 - 8 * i) % 128) if i else x
            b = rot(y, (120 - 8 * i) % 128)
            E[4 + 16 * q + i, rows, :] += jnp.where(lane < 8, a, jnp.where(lane >= 120, b, 0.0))
        return c
    lax.fori_loop(0, 18, addz, 0)
    yc = [remote(E.at[pl.ds(40, 4)], yr.at[0], send, recv, 2, "gy", 1), remote(E.at[pl.ds(4, 4)], yr.at[1], send, recv, 3, "gy", -1)]
    for c in yc:
        c.wait()
    for k in range(4):
        E[8 + k] += yr[0, k] * my
        E[36 + k] += yr[1, k] * py
    def stage(y, c):
        xs[0, pl.ds(y * 4, 4), :] = E[8 + y, pl.ds(40, 4), :]
        xs[1, pl.ds(y * 4, 4), :] = E[8 + y, pl.ds(4, 4), :]
        return c
    lax.fori_loop(0, 32, stage, 0, unroll=8)
    xc = [remote(xs.at[0], xr.at[0], send, recv, 4, "gx", 1), remote(xs.at[1], xr.at[1], send, recv, 5, "gx", -1)]
    for c in xc:
        c.wait()
    def finish(y, c):
        E[8 + y, pl.ds(8, 4), :] += xr[0, pl.ds(y * 4, 4), :] * mx
        E[8 + y, pl.ds(36, 4), :] += xr[1, pl.ds(y * 4, 4), :] * px
        for xo in range(4):
            upd[pl.ds(xo * 256 + y, 8, stride=32), :] = C[y, pl.ds(8 * xo, 8), :] + E[8 + y, pl.ds(8 + 8 * xo, 8), :]
        return c
    lax.fori_loop(0, 32, finish, 0, unroll=4)


def f32(*shape):
    return jax.ShapeDtypeStruct(shape, jnp.float32)


def vmem(*shape):
    return pltpu.VMEM(shape, jnp.float32)


def params(cid, mib):
    return pltpu.CompilerParams(collective_id=cid, has_side_effects=True, vmem_limit_bytes=mib << 20)


def share(coef, forcing, base, labels, con, chw, basis):
    return pl.pallas_call(
        share_kernel, out_shape=(f32(16, 4, 8, 128), f32(3 * 48 * 48, 128), f32(3, 7, 48, 128), f32(2, 2, 3, 5, 8, 128), f32(NP * 256, 128)),
        in_specs=[VM, VM, VM, VM, SM, SM, ANY], out_specs=(VM, VM, VM, VM, VM),
        scratch_shapes=[pltpu.SemaphoreType.DMA, vmem(8, 128), vmem(8, 8, 128), vmem(2, 3, 2, 32, 128), vmem(2, 3, 2, 32, 128), vmem(4, 3, 5, 32, 128),
                        vmem(2, 3, 5, 32, 128), vmem(2, 3, 5, 32, 128),
                        pltpu.SemaphoreType.DMA((19,)), pltpu.SemaphoreType.DMA((19,))],
        compiler_params=params(0, 20), name="share")(coef, forcing, base, labels, con, chw, basis)


def merge(T, G0, yk):
    return pl.pallas_call(
        merge_kernel, out_shape=(f32(48, 48, 128), f32(2, 7, 48, 128), f32(3, 7, 48, 128), f32(2, 2, 3, 5, 8, 128)),
        in_specs=[VM, VM, VM], out_specs=(VM, VM, VM, VM),
        scratch_shapes=[vmem(2, 3, 2, 32, 128), vmem(2, 3, 7, 8, 128), vmem(2, 2, 3, 5, 8, 128),
                        vmem(2, 5, 48, 128), vmem(2, 5, 48, 128), vmem(2, 9, 48, 128), vmem(2, 2, 2, 48, 128),
                        vmem(2, 384, 128), vmem(2, 384, 128), vmem(2, 128, 128), vmem(2, 128, 128),
                        pltpu.SemaphoreType.DMA((16,)), pltpu.SemaphoreType.DMA((16,))],
        compiler_params=params(1, 14), name="merge")(T, G0, yk)


def fold(T, C):
    return pl.pallas_call(
        fold_kernel, out_shape=f32(1024, 128), in_specs=[VM, VM], out_specs=VM,
        scratch_shapes=[vmem(52, 48, 128), vmem(2, 3, 48, 128), vmem(2, 3, 48, 128), vmem(2, 4, 48, 128),
                        vmem(2, 128, 128), vmem(2, 128, 128),
                        pltpu.SemaphoreType.DMA((6,)), pltpu.SemaphoreType.DMA((6,))],
        compiler_params=params(2, 12), name="fold")(T, C)


def prolong_kernel(live_ref, off, link, gat, buf, acc):
    live = jnp.clip(live_ref[0], 0, NP)
    acc[...] = jnp.zeros_like(acc)
    lane, sub = lanes_sub()
    ix, iy, iz = lax.axis_index("gx"), lax.axis_index("gy"), lax.axis_index("gz")

    def values(p):
        jx, jy, jz = ix + link[0, p] - 1, iy + link[1, p] - 1, iz + link[2, p] - 1
        owner = jnp.clip((jx * 4 + jy) * 8 + jz, 0, 127)
        spot = jnp.clip(link[3, p], 0, ND - 1) + 64 * lax.rem(owner, 2)
        cell = rot(gat[owner // 8, lax.rem(owner // 2, 4)], lax.rem(128 - spot, 128))
        cell = jnp.broadcast_to(cell[:, 0:1], (8, 128)) * jnp.where(p < live, 1.0, 0.0)
        ck = [jnp.broadcast_to(cell[k : k + 1, :], (8, 128)) for k in range(NB)]
        vs = {}
        for yh in range(2):
            for xo in range(2):
                t = [ck[k] * buf[pl.ds(p * 256 + 128 * xo + 8 * yh + k, 8, stride=16), :] for k in range(NB)]
                vs[yh, xo] = ((t[0] + t[1]) + (t[2] + t[3])) + ((t[4] + t[5]) + (t[6] + t[7]))
        return vs

    def body(g, c):
        pieces = [g * FEW + j for j in range(FEW)]
        every = [values(p) for p in pieces]
        for p, vs in zip(pieces, every):
            ox, oy, tile, lo = corner(off, p)
            inwin = (lane >= lo) & (lane < lo + 16)
            new = []
            for (yh, xo), v in vs.items():
                for yl in range(8):
                    r = rot(v, lax.rem(lo - 16 * yl + 128, 128))
                    spot = (tile, oy + 4 + 8 * yh + yl, pl.ds(ox + 4 + 8 * xo, 8), slice(None))
                    new.append((spot, acc[spot] + jnp.where(inwin, r, 0.0)))
            for spot, value in new:
                acc[spot] = value
        return c

    lax.fori_loop(0, (live + FEW - 1) // FEW, body, 0)


def residual_stage(E0, G, Ec, Wc, xk, E, R, K, W, gk, C, gc, inner, sem):
    lane, sub = lanes_sub()
    whole = pltpu.make_async_copy(E0, E, sem)
    whole.start()
    near = (lane < 8) | (lane >= 120)

    def unpack(n, c):
        g, xo = n // 6, lax.rem(n, 6)
        rows = pl.ds(pl.multiple_of(8 * xo, 8), 8)
        gs, cs, ks = Wc[0, g, rows, :], Wc[1, g, rows, :], G[1, g, rows, :]
        for pos in range(8):
            ey = group_row(g, pos) + 4
            s = (120 - 16 * pos) % 128
            gc[ey, rows, :] = rot(gs, s)
            gk[ey, rows, :] = rot(ks, s)
            C[ey, rows, :] = Ec[jnp.clip(ey - 4, 0, 47), rows, :] + jnp.where(near, rot(cs, s), 0.0)
        return c

    lax.fori_loop(0, 42, unpack, 0)

    whole.wait()
    for f in range(3):
        for k in range(5):
            for d, y0 in ((0, 3), (1, 40)):
                E[pl.ds((48 * f + y0 + k) * 48, 8), :] = xk[0, d, f, k]
                E[pl.ds((48 * f + y0 + k) * 48 + 40, 8), :] = xk[1, d, f, k]

    def pair(cv, kv, nc, nk):
        inside = nk > 0.0
        return jnp.where(inside, 0.5 * (kv + nk) * (cv - nc), kv * cv)

    def build(n, c):
        g, xo = 1 + n // 5, lax.rem(n, 5)
        x0 = 4 + 8 * xo
        rows = pl.ds(x0, 8)

        def row(f, cy, dx):
            return E[pl.ds((48 * f + cy - 4) * 48 + x0 + dx, 8), :]

        gf, gw = G[0, g, rows, :], G[2, g, rows, :]
        for pos in range(8):
            ey = group_row(g, pos) + 4
            s = (120 - 16 * pos) % 128
            cv, gv = C[ey, rows, :], gc[ey, rows, :]
            kv, hv = row(1, ey, 0), gk[ey, rows, :]
            cu, cd, gu, gd = rot(cv, 127), rot(cv, 1), rot(gv, 127), rot(gv, 1)
            ku, kd, hu, hd = rot(kv, 127), rot(kv, 1), rot(hv, 127), rot(hv, 1)
            last, first = lane == 127, lane == 0
            r = row(0, ey, 0)
            r = r - pair(cv, kv, jnp.where(last, gu, cu), jnp.where(last, hu, ku))
            r = r - pair(cv, kv, jnp.where(first, gd, cd), jnp.where(first, hd, kd))
            q = rot(gf, s)
            q = q - pair(gv, hv, jnp.where(last, cu, gu), jnp.where(last, ku, hu))
            q = q - pair(gv, hv, jnp.where(first, cd, gd), jnp.where(first, kd, hd))
            for dy, dx in ((-1, 0), (1, 0), (0, -1), (0, 1)):
                rr = pl.ds(x0 + dx, 8)
                r = r - pair(cv, kv, C[ey + dy, rr, :], row(1, ey + dy, dx))
                q = q - pair(gv, hv, gc[ey + dy, rr, :], gk[ey + dy, rr, :])
            head, tail = lane < 4, lane >= 124
            py, px = ey - 8, pl.ds(pl.multiple_of(8 * xo, 8), 8)
            wv, gwv = row(2, ey, 0), rot(gw, s)
            for F, inn, out in ((R, r, q), (K, kv, hv), (W, wv, gwv)):
                F[0, py, px, :] = rot(jnp.where(tail, out, inn), 4)
                F[1, py, px, :] = rot(jnp.where(head, out, inn), 124)
        return c

    lax.fori_loop(0, 25, build, 0)

    def keep(y, c):
        inner[y] = C[y + 12, pl.ds(8, 32), :]
        return c

    lax.fori_loop(0, 32, keep, 0)


def enrich_kernel(live_ref, off, E0, G, Ec, Wc, xk, out, corr, inner, E, R, K, W, gk, C, gc, cbuf, vbuf, sem):
    residual_stage(E0, G, Ec, Wc, xk, E, R, K, W, gk, C, gc, inner, sem)
    live = jnp.clip(live_ref[0], 0, NP)
    corr[...] = jnp.zeros_like(corr)
    lane, sub = lanes_sub()
    group = lane // 16
    zpos = lane % 16
    zw = zpos < 15
    zg = zpos > 0
    yup = lane < 112
    ydn = lane >= 16
    xup = sub < 7
    xdn = sub > 0
    fz = zpos.astype(jnp.float32)
    def tentf(t):
        return (t + 0.5) * (PIECE - t - 0.5) * (4.0 / (PIECE * PIECE))
    tents = {}
    for xp in range(2):
        for yp in range(2):
            tents[xp, yp] = tentf((2*sub + xp).astype(jnp.float32)) * tentf((2*group + yp).astype(jnp.float32)) * tentf(fz)
    par = [(0,0),(0,1),(1,0),(1,1)]

    def prep(p, slot):
        ox, oy, tile, lo = corner(off, p)
        active = jnp.where(p < live, 1.0, 0.0)
        got = []
        for F in (R, K, W):
            d = {}
            for xp, yp in par:
                a = None
                for yh in range(8):
                    row = F[tile, oy + 2*yh + yp, pl.ds(ox + xp, 8, stride=2), :]
                    r = rot(row, lax.rem(16*yh - lo + 128, 128))
                    a = r if a is None else jnp.where(group == yh, r, a)
                d[xp, yp] = a
            got.append(d)
        r, k, w = got
        for i, (xp, yp) in enumerate(par):
            kc = k[xp, yp]
            nbs = [
                (rot(kc, 127), zw), (rot(kc, 1), zg),
                (k[xp, 1-yp], None),
                (rot(k[xp, 1-yp], 16 if yp == 0 else 112), ydn if yp == 0 else yup),
                (k[1-xp, yp], None),
                (rot(k[1-xp, yp], 1 if xp == 0 else 7, 0), xdn if xp == 0 else xup),
            ]
            diag = None
            cs = []
            inside = kc > 0.0
            for nb, m in nbs:
                ok = nb > 0.0
                if m is not None:
                    ok = ok & m
                face = jnp.where(ok, 0.5 * (kc + nb), kc)
                cs.append(jnp.where(ok & inside, face, 0.0))
                diag = face if diag is None else diag + face
            inv = jnp.where(inside, OMEGA / jnp.where(inside, diag, 1.0), 0.0)
            for j, cj in enumerate(cs):
                cbuf[slot, pl.ds((i*6 + j)*8, 8), :] = cj * inv
            b1 = r[xp, yp] * inv * active
            vbuf[slot, pl.ds(i*8, 8), :] = b1
            vbuf[slot, pl.ds((4+i)*8, 8), :] = b1 * w[xp, yp]

    def sweep_piece(vs, slot):
        res = []
        for s in range(2):
            v = {par[i]: vs[s*4+i] for i in range(4)}
            for i, (xp, yp) in enumerate(par):
                c = [cbuf[slot, pl.ds((i*6 + j)*8, 8), :] for j in range(6)]
                vc = v[xp, yp]
                t0 = vbuf[slot, pl.ds((4*s+i)*8, 8), :] + (1.0 - OMEGA) * vc
                t1 = c[0] * rot(vc, 127) + c[1] * rot(vc, 1)
                t2 = c[2] * v[xp, 1-yp] + c[3] * rot(v[xp, 1-yp], 16 if yp == 0 else 112)
                t3 = c[4] * v[1-xp, yp] + c[5] * rot(v[1-xp, yp], 1 if xp == 0 else 7, 0)
                res.append((t0 + t1) + (t2 + t3))
        return res

    idxs = [16*(4*yh2 + group//2) + zpos for yh2 in range(2)]
    gpar = (group % 2) == 0

    def body(g, c):
        for slot in range(PAIR):
            prep(g*PAIR + slot, slot)
        init = tuple(vbuf[slot, pl.ds(n*8, 8), :] for slot in range(PAIR) for n in range(8))
        def sweep(_, vs):
            o = []
            for slot in range(PAIR):
                o += sweep_piece(vs[slot*8:slot*8+8], slot)
            return tuple(o)
        vs = lax.fori_loop(0, SWEEPS - 1, sweep, init)
        for slot in range(PAIR):
            p = g*PAIR + slot
            ox, oy, tile, lo = corner(off, p)
            inwin = (lane >= lo) & (lane < lo + 16)
            v = vs[slot*8:slot*8+8]
            for s in range(2):
                for xp in range(2):
                    for yh2 in range(2):
                        e = jnp.take_along_axis(v[s*4 + 2*xp], idxs[yh2], axis=1)
                        o = jnp.take_along_axis(v[s*4 + 2*xp + 1], idxs[yh2], axis=1)
                        out[pl.ds(p*64 + 4*xp + 2*yh2 + s, 8, stride=8), :] = jnp.where(gpar, e, o)
            for i, (xp, yp) in enumerate(par):
                sp = tents[xp, yp] * (v[i] + v[4+i])
                new = []
                for yh in range(8):
                    rr = jnp.where(inwin, rot(sp, lax.rem(lo - 16*yh + 128, 128)), 0.0)
                    spot = (tile, oy + 4 + 2*yh + yp, pl.ds(ox + 4 + xp, 8, stride=2), slice(None))
                    new.append((spot, corr[spot] + rr))
                for spot, value in new:
                    corr[spot] = value
        return c
    ng = (live + PAIR - 1) // PAIR
    lax.fori_loop(0, ng, body, 0)
    def zero(p, c):
        out[pl.ds(p*64, 64), :] = jnp.zeros((64, 128), jnp.float32)
        return c
    lax.fori_loop(ng*PAIR, NP, zero, 0)


def prolong(live, off, link, gat, basis):
    return pl.pallas_call(
        prolong_kernel, out_shape=f32(2, 52, 48, 128), in_specs=[SM, SM, SM, VM, VM], out_specs=VM,
        compiler_params=pltpu.CompilerParams(vmem_limit_bytes=14 << 20), name="prolong")(live, off, link, gat, basis)


def enrich(live, off, E, G, Ec, Wc, xk):
    return pl.pallas_call(
        enrich_kernel, out_shape=(f32(NP * 64, 128), f32(2, 52, 48, 128), f32(32, 32, 128)),
        in_specs=[SM, SM, pl.BlockSpec(memory_space=pl.ANY), VM, VM, VM, VM], out_specs=(VM, VM, VM),
        scratch_shapes=[vmem(3 * 48 * 48, 128), vmem(2, 40, 40, 128), vmem(2, 40, 40, 128), vmem(2, 40, 40, 128),
                        vmem(56, 48, 128), vmem(56, 48, 128), vmem(56, 48, 128), vmem(PAIR, 192, 128), vmem(PAIR, 64, 128), pltpu.SemaphoreType.DMA],
        compiler_params=pltpu.CompilerParams(vmem_limit_bytes=30 << 20), name="enrich")(live, off, E, G, Ec, Wc, xk)


def basis_rows(rb):
    return rb.reshape(NP, NB, 32, 128).transpose(0, 2, 1, 3).reshape(NP * 256, 128)


def out_basis(o):
    return o.reshape(NP, 32, 2, 128).transpose(0, 2, 1, 3).reshape(1, 1, 1, NP, 2, 4096)


def local(forcing, kappa_base, labels, contrast, channel_weight, coarse_coef, source_link, offsets, live_pieces, resident_bases):
    live = live_pieces.reshape(1)
    off = offsets[0, 0].transpose(2, 0, 1)
    link = source_link[0, 0, 0].T
    gat, E, G0, yk, held = share(
        coarse_coef[0, 0, 0].T, forcing.reshape(1024, 128), kappa_base.reshape(1024, 128), labels.reshape(1024, 128),
        contrast, channel_weight, basis_rows(resident_bases))
    T = prolong(live, off, link, gat, held)
    Ec, Wc, G, xk = merge(T, G0, yk)
    out, corr, inner = enrich(live, off, E, G, Ec, Wc, xk)
    return fold(corr, inner).reshape(32, 32, 128), out_basis(out)


def solution(mesh):
    return jax.shard_map(
        local,
        mesh=mesh,
        in_specs=(
            P("gx", "gy", "gz"),
            P("gx", "gy", "gz"),
            P("gx", "gy", "gz"),
            P(),
            P(),
            P("gx", "gy", "gz", None, None),
            P("gx", "gy", "gz", None, None),
            P("gx", "gy", "gz", None, None),
            P("gx", "gy", "gz"),
            P("gx", "gy", "gz", None, None, None),
        ),
        out_specs=(P("gx", "gy", "gz"), P("gx", "gy", "gz", None, None, None)),
        check_vma=False,
    )
```

profile of v0, /device:TPU:41, one launch (start us, length us, event | category | flops | bytes accessed | tf_op | source)
XLA Modules:
  0.0 134.2 jit_solution(2881133112122195995)
XLA Ops:
  1.3 0.0 copy-start
  1.3 2.5 %copy-done = f32[1,1,1,40,8,4096]{5,4,3,2,1,0:T(8,128)S(1)} copy-done((f32[1,1,1,40,8,4096]{5,4,3,2,1,0:T(8,128)S(1)}, f32[1,1,1,40,8,4096]{5,4,3,2,1,0:T(8,128)}, u32[]{:S(2)}) %copy-start) | copy-done | bytes 5242904
  3.8 0.0 copy-start.1
  3.8 1.0 copy-done.1
  4.8 0.0 copy-start.2
  4.8 1.0 copy-done.2
  5.9 0.0 copy-start.3
  5.9 1.0 copy-done.3
  6.9 0.0 copy-start.5
  6.9 0.7 copy-done.5
  7.6 0.0 copy-start.7
  7.6 0.7 copy-done.7
  8.2 0.0 copy-start.8
  8.2 0.7 copy-done.8
  8.9 0.0 copy-start.4
  8.9 0.0 copy-start.6
  8.9 26.1 %share.1 = (f32[16,4,8,128]{3,2,1,0:T(8,128)S(1)}, f32[6912,128]{1,0:T(8,128)S(1)}, f32[3,7,48,128]{3,2,1,0:T(8,128)S(1)}, f32[2,2,3,5,8,128]{5,4,3,2,1,0:T(8,128)S(1)}, f32[10240,128]{1,0:T(8,128)S(1)}) custom-call(f32[8,64]{1,0:T(8,128)S(1)} %bitcast.33, f32[1024,128]{1,0:T(8,128)S(1)} %bitcast.28, f32[1024,128]{1,0:T(8,128)S(1)} %bitcast.29, ...), custom_call_target="tpu_custom_call" | custom-call | tf_op jit(solution)/shard_map/share/pallas_call | solution.py:390
  35.0 0.0 copy-done.4
  35.0 0.0 copy-done.6
  35.0 1.4 %prolong.1.T = f32[2,52,48,128]{3,2,1,0:T(8,128)S(1)} custom-call(s32[1]{0:T(128)} %bitcast.24.live_ref, s32[3,1,40]{2,1,0:T(1,128)S(1)} %bitcast.31, s32[4,40]{1,0:T(4,128)S(1)} %bitcast.34, f32[16,4,8,128]{3,2,1,0:T(8,128)S(1)} %get-tuple-element.15.gat, f32[10240,128]{1,0:T(8,128)S(1)} %get-tuple-element.16.buf), custom_call_target="tpu_custom_call" | custom-call | tf_op jit(solution)/shard_map/prolong/pallas_call | solution.py:653
  36.4 31.5 %merge.1 = (f32[48,48,128]{2,1,0:T(8,128)S(1)}, f32[2,7,48,128]{3,2,1,0:T(8,128)S(1)}, f32[3,7,48,128]{3,2,1,0:T(8,128)S(1)}, f32[2,2,3,5,8,128]{5,4,3,2,1,0:T(8,128)S(1)}) custom-call(f32[2,52,48,128]{3,2,1,0:T(8,128)S(1)} %prolong.1.T, f32[3,7,48,128]{3,2,1,0:T(8,128)S(1)} %get-tuple-element.17.G0, f32[2,2,3,5,8,128]{5,4,3,2,1,0:T(8,128)S(1)} %get-tuple-element.18.yk), custom_call_target="tpu_custom_call" | custom-call | tf_op jit(solution)/shard_map/merge/pallas_call | solution.py:400
  67.9 20.8 %enrich.1 = (f32[2560,128]{1,0:T(8,128)}, f32[2,52,48,128]{3,2,1,0:T(8,128)S(1)}, f32[32,32,128]{2,1,0:T(8,128)S(1)}) custom-call(s32[1]{0:T(128)} %bitcast.25.live_ref, s32[3,1,40]{2,1,0:T(1,128)S(1)} %bitcast.32, f32[6912,128]{1,0:T(8,128)S(1)} %get-tuple-element.14.E0, f32[3,7,48,128]{3,2,1,0:T(8,128)S(1)} %get-tuple-element.19.G, ...), custom_call_target="tpu_custom_call" | custom-call | tf_op jit(solution)/shard_map/enrich/pallas_call | solution.py:659
  88.7 44.7 %fold.1 = f32[1024,128]{1,0:T(8,128)S(1)} custom-call(f32[2,52,48,128]{3,2,1,0:T(8,128)S(1)} %get-tuple-element.23.T, f32[32,32,128]{2,1,0:T(8,128)S(1)} %get-tuple-element.24.C), custom_call_target="tpu_custom_call" | custom-call | tf_op jit(solution)/shard_map/fold/pallas_call | solution.py:411
  133.4 0.8 copy.15
Async XLA Ops:
  1.3 2.5 %copy-start = (f32[1,1,1,40,8,4096]{5,4,3,2,1,0:T(8,128)S(1)}, f32[1,1,1,40,8,4096]{5,4,3,2,1,0:T(8,128)}, u32[]{:S(2)}) copy-start(f32[1,1,1,40,8,4096]{5,4,3,2,1,0:T(8,128)} %param.19) | copy-start | bytes 15728644
  3.8 1.0 copy-start.1
  4.8 1.0 copy-start.2
  5.9 1.0 copy-start.3
  6.9 0.7 copy-start.5
  7.6 0.7 copy-start.7
  8.2 0.7 copy-start.8
  8.9 26.1 %copy-start.4 = (s32[1,1,1,40,3]{3,2,4,1,0:T(1,128)S(1)}, s32[1,1,1,40,3]{3,2,4,1,0:T(1,128)}, u32[]{:S(2)}) copy-start(s32[1,1,1,40,3]{3,2,4,1,0:T(1,128)} %param.17) | copy-start | bytes 1444
  8.9 26.1 %copy-start.6 = (s32[1,1,1,40,4]{3,4,2,1,0:T(4,128)S(1)}, s32[1,1,1,40,4]{3,4,2,1,0:T(4,128)}, u32[]{:S(2)}) copy-start(s32[1,1,1,40,4]{3,4,2,1,0:T(4,128)} %param.16) | copy-start | bytes 1924
where the time goes:
time: 137 us; the launch traced here: 134 us
  Pallas kernels  124 us (91%)
  local copies, waits for them, and re-layouts  8.4 us (6%)
    pallas_call x1, Pallas kernels, fold(): pl.pallas_call(fold_kernel, out_shape=f32(1024, 128), in_specs=[VM, VM],...  44.7 us
    pallas_call x1, Pallas kernels, merge(): pl.pallas_call(merge_kernel, out_shape=(f32(48, 48, 128), f32(2, 7, 48, 1...  31.5 us
    pallas_call x1, Pallas kernels, share(): pl.pallas_call(share_kernel, out_shape=(f32(16, 4, 8, 128), f32(3 * 48 *...  26.1 us
    pallas_call x1, Pallas kernels, enrich(): pl.pallas_call(enrich_kernel, out_shape=(f32(NP * 64, 128), f32(2, 52, 48...  20.8 us
    unnamed x19, local copies, waits for them, and re-layouts  8.4 us

commit v1 on v0

--- a/solution.py
+++ b/solution.py
@@ -61,16 +61,22 @@
     return 8 * g - 4 + pos
 
 
-def share_kernel(coef, forcing, base, labels, con, chw, basis, gat, E, G, yk, held, bsem, tile, col, zs, zr, yr, xs, xr, send, recv):
+def share_kernel(coef, forcing0, base0, labels0, con, chw, basis, gat, E, G, yk, held, bsem, forcing, base, labels, isem, tile, col, zs, zr, yr, xs, xr, send, recv):
     ix, iy, iz = lax.axis_index("gx"), lax.axis_index("gy"), lax.axis_index("gz")
     lane, sub = lanes_sub()
     tile[...] = jnp.zeros_like(tile)
     tile[0:8, 0:64] = coef[...]
+    fields = [pltpu.make_async_copy(a, b, isem.at[i]) for i, (a, b) in enumerate(((forcing0, forcing), (base0, base), (labels0, labels)))]
+    for c in fields:
+        c.start()
     fetch = pltpu.make_async_copy(basis, held, bsem)
     fetch.start()
     greet([("gz", s) for s in range(1, 8)] + [("gy", s) for s in range(1, 4)] + [("gx", s) for s in range(1, 4)])
     g1 = [remote(tile, col.at[iz], send, recv, s - 1, "gz", s) for s in range(1, 8)]
     col[iz] = tile[...]
+
+    for c in fields:
+        c.wait()
 
     def fill(x, c):
         for yo in range(4):
@@ -92,18 +98,6 @@
         return c
 
     lax.fori_loop(0, 32, fill, 0, unroll=2)
-    xm = [remote(xs.at[0], xr.at[0], send, recv, 7, "gx", 1), remote(xs.at[1], xr.at[1], send, recv, 8, "gx", -1)]
-
-    def stagey(n, c):
-        f, k = n // 5, lax.rem(n, 5)
-        zs_hi = (48 * f + 35 + k) * 48 + 8
-        zs_lo = (48 * f + 8 + k) * 48 + 8
-        yr[0, f, k] = E[pl.ds(pl.multiple_of(zs_hi, 8), 32), :]
-        yr[1, f, k] = E[pl.ds(pl.multiple_of(zs_lo, 8), 32), :]
-        return c
-
-    lax.fori_loop(0, 15, stagey, 0)
-    yc = [remote(yr.at[0], yr.at[2], send, recv, 9, "gy", 1), remote(yr.at[1], yr.at[3], send, recv, 10, "gy", -1)]
     lane8 = lane // 8
 
     def packz(n, c):
@@ -121,6 +115,18 @@
 
     lax.fori_loop(0, 24, packz, 0)
     zc = [remote(zs.at[0], zr.at[0], send, recv, 11, "gz", 1), remote(zs.at[1], zr.at[1], send, recv, 12, "gz", -1)]
+    xm = [remote(xs.at[0], xr.at[0], send, recv, 7, "gx", 1), remote(xs.at[1], xr.at[1], send, recv, 8, "gx", -1)]
+
+    def stagey(n, c):
+        f, k = n // 5, lax.rem(n, 5)
+        zs_hi = (48 * f + 35 + k) * 48 + 8
+        zs_lo = (48 * f + 8 + k) * 48 + 8
+        yr[0, f, k] = E[pl.ds(pl.multiple_of(zs_hi, 8), 32), :]
+        yr[1, f, k] = E[pl.ds(pl.multiple_of(zs_lo, 8), 32), :]
+        return c
+
+    lax.fori_loop(0, 15, stagey, 0)
+    yc = [remote(yr.at[0], yr.at[2], send, recv, 9, "gy", 1), remote(yr.at[1], yr.at[3], send, recv, 10, "gy", -1)]
     for c in g1:
         c.wait()
     mine = ix * 4 + iy
@@ -148,6 +154,17 @@
         return c
 
     lax.fori_loop(0, 15, addy, 0)
+    for c in xm:
+        c.wait()
+
+    def addx(n, c):
+        f, k = n // 5, lax.rem(n, 5)
+        for yo in range(4):
+            E[pl.ds((48 * f + 8 + 8 * yo) * 48 + 3 + k, 8, stride=48), :] = xr[0, f, k, pl.ds(8 * yo, 8), :] * mx
+            E[pl.ds((48 * f + 8 + 8 * yo) * 48 + 40 + k, 8, stride=48), :] = xr[1, f, k, pl.ds(8 * yo, 8), :] * px
+        return c
+
+    lax.fori_loop(0, 15, addx, 0)
     for c in zc:
         c.wait()
     lane16 = lane // 16
@@ -170,17 +187,6 @@
         return c
 
     lax.fori_loop(0, 12, windows, 0)
-    for c in xm:
-        c.wait()
-
-    def addx(n, c):
-        f, k = n // 5, lax.rem(n, 5)
-        for yo in range(4):
-            E[pl.ds((48 * f + 8 + 8 * yo) * 48 + 3 + k, 8, stride=48), :] = xr[0, f, k, pl.ds(8 * yo, 8), :] * mx
-            E[pl.ds((48 * f + 8 + 8 * yo) * 48 + 40 + k, 8, stride=48), :] = xr[1, f, k, pl.ds(8 * yo, 8), :] * px
-        return c
-
-    lax.fori_loop(0, 15, addx, 0)
     for c in g3:
         c.wait()
     fetch.wait()
@@ -208,10 +214,15 @@
     low = lax.rem(lane, 16) < 8
     E[3] = jnp.zeros((48, 128), jnp.float32)
     E[44] = jnp.zeros((48, 128), jnp.float32)
+    side = jnp.zeros((41, 8, 128), jnp.float32)
+    E[pl.ds(4, 41), pl.ds(0, 8), :] = side
+    E[pl.ds(4, 41), pl.ds(40, 8), :] = side
+    W[:, :, pl.ds(0, 8), :] = jnp.zeros((2, 7, 8, 128), jnp.float32)
+    W[:, :, pl.ds(40, 8), :] = jnp.zeros((2, 7, 8, 128), jnp.float32)
 
     def build(n, c):
-        g, xo = 1 + n // 6, lax.rem(n, 6)
-        rows = pl.ds(pl.multiple_of(8 * xo, 8), 8)
+        g, xo = 1 + n // 5, lax.rem(n, 5)
+        rows, near = pl.ds(4 + 8 * xo, 8), pl.ds(pl.multiple_of(8 * xo, 8), 8)
         nxt, prv, own = None, None, None
         for pos in range(8):
             ey = 8 * g - 4 + pos
@@ -225,12 +236,12 @@
             else:
                 hit = lane16 == pos
                 nxt, prv, own = jnp.where(hit, s0, nxt), jnp.where(hit, s1, prv), jnp.where(hit, rm, own)
-        zs[0, g - 1, rows, :] = nxt
-        zs[1, g - 1, rows, :] = prv
+        zs[0, g - 1, near, :] = nxt
+        zs[1, g - 1, near, :] = prv
         W[0, g, rows, :] = own
         return c
 
-    lax.fori_loop(0, 30, build, 0)
+    lax.fori_loop(0, 25, build, 0)
     zc = [remote(zs.at[0], zr.at[0], send, recv, 2, "gz", 1), remote(zs.at[1], zr.at[1], send, recv, 3, "gz", -1)]
     yc = [remote(E.at[pl.ds(35, 9)], yr.at[0], send, recv, 0, "gy", 1), remote(E.at[pl.ds(4, 9)], yr.at[1], send, recv, 1, "gy", -1)]
     my, py = edges("gy")
@@ -263,13 +274,13 @@
     for c in zc:
         c.wait()
     def windows(n, c):
-        g, xo = n // 6, lax.rem(n, 6)
-        rows = pl.ds(pl.multiple_of(8 * xo, 8), 8)
-        x, y = zr[0, g, rows, :] * mz, zr[1, g, rows, :] * pz
+        g, xo = n // 5, lax.rem(n, 5)
+        rows, near = pl.ds(4 + 8 * xo, 8), pl.ds(pl.multiple_of(8 * xo, 8), 8)
+        x, y = zr[0, g, near, :] * mz, zr[1, g, near, :] * pz
         W[0, g + 1, rows, :] += jnp.where(low, x, y)
         W[1, g + 1, rows, :] = jnp.where(low, y, x)
         return c
-    lax.fori_loop(0, 30, windows, 0)
+    lax.fori_loop(0, 25, windows, 0, unroll=5)
     wc = [remote(W.at[:, pl.ds(4, 2)], yw.at[0], send, recv, 6, "gy", 1), remote(W.at[:, pl.ds(1, 2)], yw.at[1], send, recv, 7, "gy", -1)]
     for c in wc:
         c.wait()
@@ -319,8 +330,8 @@
     lane8 = lane // 8
 
     def build(n, c):
-        q, xo = n // 6, lax.rem(n, 6)
-        rows = pl.ds(pl.multiple_of(8 * xo, 8), 8)
+        q, xo = n // 5, lax.rem(n, 5)
+        rows, near = pl.ds(4 + 8 * xo, 8), pl.ds(pl.multiple_of(8 * xo, 8), 8)
         nxt, prv = None, None
         for i in range(16):
             ey = 4 + 16 * q + i
@@ -330,11 +341,11 @@
             lo = rot(m, (8 * i + 8) % 128)
             nxt = hi if i == 0 else jnp.where(lane8 == i, hi, nxt)
             prv = lo if i == 0 else jnp.where(lane8 == i, lo, prv)
-        zs[0, q, rows, :] = nxt
-        zs[1, q, rows, :] = prv
-        return c
-
-    lax.fori_loop(0, 18, build, 0)
+        zs[0, q, near, :] = nxt
+        zs[1, q, near, :] = prv
+        return c
+
+    lax.fori_loop(0, 15, build, 0)
     zc = [remote(zs.at[0], zr.at[0], send, recv, 0, "gz", 1), remote(zs.at[1], zr.at[1], send, recv, 1, "gz", -1)]
     my, py = edges("gy")
     mz, pz = edges("gz")
@@ -342,15 +353,15 @@
     for c in zc:
         c.wait()
     def addz(n, c):
-        q, xo = n // 6, lax.rem(n, 6)
-        rows = pl.ds(pl.multiple_of(8 * xo, 8), 8)
-        x, y = zr[0, q, rows, :] * mz, zr[1, q, rows, :] * pz
+        q, xo = n // 5, lax.rem(n, 5)
+        rows, near = pl.ds(4 + 8 * xo, 8), pl.ds(pl.multiple_of(8 * xo, 8), 8)
+        x, y = zr[0, q, near, :] * mz, zr[1, q, near, :] * pz
         for i in range(16):
             a = rot(x, (128 - 8 * i) % 128) if i else x
             b = rot(y, (120 - 8 * i) % 128)
             E[4 + 16 * q + i, rows, :] += jnp.where(lane < 8, a, jnp.where(lane >= 120, b, 0.0))
         return c
-    lax.fori_loop(0, 18, addz, 0)
+    lax.fori_loop(0, 15, addz, 0)
     yc = [remote(E.at[pl.ds(40, 4)], yr.at[0], send, recv, 2, "gy", 1), remote(E.at[pl.ds(4, 4)], yr.at[1], send, recv, 3, "gy", -1)]
     for c in yc:
         c.wait()
@@ -389,11 +400,12 @@
 def share(coef, forcing, base, labels, con, chw, basis):
     return pl.pallas_call(
         share_kernel, out_shape=(f32(16, 4, 8, 128), f32(3 * 48 * 48, 128), f32(3, 7, 48, 128), f32(2, 2, 3, 5, 8, 128), f32(NP * 256, 128)),
-        in_specs=[VM, VM, VM, VM, SM, SM, ANY], out_specs=(VM, VM, VM, VM, VM),
-        scratch_shapes=[pltpu.SemaphoreType.DMA, vmem(8, 128), vmem(8, 8, 128), vmem(2, 3, 2, 32, 128), vmem(2, 3, 2, 32, 128), vmem(4, 3, 5, 32, 128),
+        in_specs=[VM, ANY, ANY, ANY, SM, SM, ANY], out_specs=(VM, VM, VM, VM, VM),
+        scratch_shapes=[pltpu.SemaphoreType.DMA, vmem(1024, 128), vmem(1024, 128), pltpu.VMEM((1024, 128), jnp.int32), pltpu.SemaphoreType.DMA((3,)),
+                        vmem(8, 128), vmem(8, 8, 128), vmem(2, 3, 2, 32, 128), vmem(2, 3, 2, 32, 128), vmem(4, 3, 5, 32, 128),
                         vmem(2, 3, 5, 32, 128), vmem(2, 3, 5, 32, 128),
                         pltpu.SemaphoreType.DMA((19,)), pltpu.SemaphoreType.DMA((19,))],
-        compiler_params=params(0, 20), name="share")(coef, forcing, base, labels, con, chw, basis)
+        compiler_params=params(0, 41), name="share")(coef, forcing, base, labels, con, chw, basis)
 
 
 def merge(T, G0, yk):
@@ -401,7 +413,7 @@
         merge_kernel, out_shape=(f32(48, 48, 128), f32(2, 7, 48, 128), f32(3, 7, 48, 128), f32(2, 2, 3, 5, 8, 128)),
         in_specs=[VM, VM, VM], out_specs=(VM, VM, VM, VM),
         scratch_shapes=[vmem(2, 3, 2, 32, 128), vmem(2, 3, 7, 8, 128), vmem(2, 2, 3, 5, 8, 128),
-                        vmem(2, 5, 48, 128), vmem(2, 5, 48, 128), vmem(2, 9, 48, 128), vmem(2, 2, 2, 48, 128),
+                        vmem(2, 5, 40, 128), vmem(2, 5, 40, 128), vmem(2, 9, 48, 128), vmem(2, 2, 2, 48, 128),
                         vmem(2, 384, 128), vmem(2, 384, 128), vmem(2, 128, 128), vmem(2, 128, 128),
                         pltpu.SemaphoreType.DMA((16,)), pltpu.SemaphoreType.DMA((16,))],
         compiler_params=params(1, 14), name="merge")(T, G0, yk)
@@ -410,7 +422,7 @@
 def fold(T, C):
     return pl.pallas_call(
         fold_kernel, out_shape=f32(1024, 128), in_specs=[VM, VM], out_specs=VM,
-        scratch_shapes=[vmem(52, 48, 128), vmem(2, 3, 48, 128), vmem(2, 3, 48, 128), vmem(2, 4, 48, 128),
+        scratch_shapes=[vmem(52, 48, 128), vmem(2, 3, 40, 128), vmem(2, 3, 40, 128), vmem(2, 4, 48, 128),
                         vmem(2, 128, 128), vmem(2, 128, 128),
                         pltpu.SemaphoreType.DMA((6,)), pltpu.SemaphoreType.DMA((6,))],
         compiler_params=params(2, 12), name="fold")(T, C)
@@ -676,9 +688,9 @@
     live = live_pieces.reshape(1)
     off = offsets[0, 0].transpose(2, 0, 1)
     link = source_link[0, 0, 0].T
-    gat, E, G0, yk, held = share(
+    gat, E, G0, yk, held = share(*(pltpu.with_memory_space_constraint(v, pltpu.HBM) for v in (
         coarse_coef[0, 0, 0].T, forcing.reshape(1024, 128), kappa_base.reshape(1024, 128), labels.reshape(1024, 128),
-        contrast, channel_weight, basis_rows(resident_bases))
+        contrast, channel_weight, basis_rows(resident_bases))))
     T = prolong(live, off, link, gat, held)
     Ec, Wc, G, xk = merge(T, G0, yk)
     out, corr, inner = enrich(live, off, E, G, Ec, Wc, xk)

time: 137 us -> 126 us (0.920)
  the two profiles are of different devices: /device:TPU:41 before, /device:TPU:10 now
where the time goes in v1:
time: 126 us; the launch traced here: 127 us
  Pallas kernels  124 us (98%)
  between operations  1.35 us (1%)
    pallas_call x1, Pallas kernels, fold(): pl.pallas_call(fold_kernel, out_shape=f32(1024, 128), in_specs=[VM, VM],...  45.7 us
    pallas_call x1, Pallas kernels, share(): pl.pallas_call(share_kernel, out_shape=(f32(16, 4, 8, 128), f32(3 * 48 *...  30.1 us
    pallas_call x1, Pallas kernels, merge(): pl.pallas_call(merge_kernel, out_shape=(f32(48, 48, 128), f32(2, 7, 48, 1...  26.4 us
    pallas_call x1, Pallas kernels, enrich(): pl.pallas_call(enrich_kernel, out_shape=(f32(NP * 64, 128), f32(2, 52, 48...  20.8 us

profile of v1, /device:TPU:10, one launch (start us, length us, event | category | flops | bytes accessed | tf_op | source)
XLA Modules:
  0.0 126.6 jit_solution(5839133859963434358)
XLA Ops:
  1.3 0.0 copy-start
  1.3 0.0 copy-start.1
  1.3 30.1 %share.1 = (f32[16,4,8,128]{3,2,1,0:T(8,128)S(1)}, f32[6912,128]{1,0:T(8,128)S(1)}, f32[3,7,48,128]{3,2,1,0:T(8,128)S(1)}, f32[2,2,3,5,8,128]{5,4,3,2,1,0:T(8,128)S(1)}, f32[10240,128]{1,0:T(8,128)S(1)}) custom-call(f32[8,64]{1,0:T(8,128)} %bitcast.34, f32[1024,128]{1,0:T(8,128)} %bitcast.31, f32[1024,128]{1,0:T(8,128)} %bitcast.32, s32[1024,128]{1,0:T(8,128)} %bitcast.33, ...), custom_call_target="tpu_custom_call" | custom-call | tf_op jit(solution)/shard_map/share/pallas_call | solution.py:401
  31.4 0.0 copy-done
  31.4 0.0 copy-done.1
  31.5 1.4 %prolong.1.T = f32[2,52,48,128]{3,2,1,0:T(8,128)S(1)} custom-call(s32[1]{0:T(128)} %bitcast.24.live_ref, s32[3,1,40]{2,1,0:T(1,128)S(1)} %bitcast.27, s32[4,40]{1,0:T(4,128)S(1)} %bitcast.29, f32[16,4,8,128]{3,2,1,0:T(8,128)S(1)} %get-tuple-element.15.gat, f32[10240,128]{1,0:T(8,128)S(1)} %get-tuple-element.16.buf), custom_call_target="tpu_custom_call" | custom-call | tf_op jit(solution)/shard_map/prolong/pallas_call | solution.py:665
  32.9 26.4 %merge.1 = (f32[48,48,128]{2,1,0:T(8,128)S(1)}, f32[2,7,48,128]{3,2,1,0:T(8,128)S(1)}, f32[3,7,48,128]{3,2,1,0:T(8,128)S(1)}, f32[2,2,3,5,8,128]{5,4,3,2,1,0:T(8,128)S(1)}) custom-call(f32[2,52,48,128]{3,2,1,0:T(8,128)S(1)} %prolong.1.T, f32[3,7,48,128]{3,2,1,0:T(8,128)S(1)} %get-tuple-element.17.G0, f32[2,2,3,5,8,128]{5,4,3,2,1,0:T(8,128)S(1)} %get-tuple-element.18.yk), custom_call_target="tpu_custom_call" | custom-call | tf_op jit(solution)/shard_map/merge/pallas_call | solution.py:412
  59.2 20.8 %enrich.1 = (f32[2560,128]{1,0:T(8,128)}, f32[2,52,48,128]{3,2,1,0:T(8,128)S(1)}, f32[32,32,128]{2,1,0:T(8,128)S(1)}) custom-call(s32[1]{0:T(128)} %bitcast.25.live_ref, s32[3,1,40]{2,1,0:T(1,128)S(1)} %bitcast.28, f32[6912,128]{1,0:T(8,128)S(1)} %get-tuple-element.14.E0, f32[3,7,48,128]{3,2,1,0:T(8,128)S(1)} %get-tuple-element.19.G, ...), custom_call_target="tpu_custom_call" | custom-call | tf_op jit(solution)/shard_map/enrich/pallas_call | solution.py:671
  80.0 45.7 %fold.1 = f32[1024,128]{1,0:T(8,128)S(1)} custom-call(f32[2,52,48,128]{3,2,1,0:T(8,128)S(1)} %get-tuple-element.23.T, f32[32,32,128]{2,1,0:T(8,128)S(1)} %get-tuple-element.24.C), custom_call_target="tpu_custom_call" | custom-call | tf_op jit(solution)/shard_map/fold/pallas_call | solution.py:423
  125.8 0.8 copy.15
Async XLA Ops:
  1.3 30.2 %copy-start = (s32[1,1,1,40,3]{3,2,4,1,0:T(1,128)S(1)}, s32[1,1,1,40,3]{3,2,4,1,0:T(1,128)}, u32[]{:S(2)}) copy-start(s32[1,1,1,40,3]{3,2,4,1,0:T(1,128)} %param.17) | copy-start | bytes 1444
  1.3 30.2 %copy-start.1 = (s32[1,1,1,40,4]{3,4,2,1,0:T(4,128)S(1)}, s32[1,1,1,40,4]{3,4,2,1,0:T(4,128)}, u32[]{:S(2)}) copy-start(s32[1,1,1,40,4]{3,4,2,1,0:T(4,128)} %param.16) | copy-start | bytes 1924

commit v2 on v1

--- a/solution.py
+++ b/solution.py
@@ -8,7 +8,7 @@
 ND = 64
 PIECE=16; NB=8; NP=40; SWEEPS=20
 OMEGA = 2.0/3.0
-PAIR = 8
+PAIR = 10
 FEW = 8
 VM = pl.BlockSpec(memory_space=pltpu.VMEM)
 SM = pl.BlockSpec(memory_space=pltpu.SMEM)
@@ -98,6 +98,18 @@
         return c
 
     lax.fori_loop(0, 32, fill, 0, unroll=2)
+    xm = [remote(xs.at[0], xr.at[0], send, recv, 7, "gx", 1), remote(xs.at[1], xr.at[1], send, recv, 8, "gx", -1)]
+
+    def stagey(n, c):
+        f, k = n // 5, lax.rem(n, 5)
+        zs_hi = (48 * f + 35 + k) * 48 + 8
+        zs_lo = (48 * f + 8 + k) * 48 + 8
+        yr[0, f, k] = E[pl.ds(pl.multiple_of(zs_hi, 8), 32), :]
+        yr[1, f, k] = E[pl.ds(pl.multiple_of(zs_lo, 8), 32), :]
+        return c
+
+    lax.fori_loop(0, 15, stagey, 0)
+    yc = [remote(yr.at[0], yr.at[2], send, recv, 9, "gy", 1), remote(yr.at[1], yr.at[3], send, recv, 10, "gy", -1)]
     lane8 = lane // 8
 
     def packz(n, c):
@@ -115,18 +127,6 @@
 
     lax.fori_loop(0, 24, packz, 0)
     zc = [remote(zs.at[0], zr.at[0], send, recv, 11, "gz", 1), remote(zs.at[1], zr.at[1], send, recv, 12, "gz", -1)]
-    xm = [remote(xs.at[0], xr.at[0], send, recv, 7, "gx", 1), remote(xs.at[1], xr.at[1], send, recv, 8, "gx", -1)]
-
-    def stagey(n, c):
-        f, k = n // 5, lax.rem(n, 5)
-        zs_hi = (48 * f + 35 + k) * 48 + 8
-        zs_lo = (48 * f + 8 + k) * 48 + 8
-        yr[0, f, k] = E[pl.ds(pl.multiple_of(zs_hi, 8), 32), :]
-        yr[1, f, k] = E[pl.ds(pl.multiple_of(zs_lo, 8), 32), :]
-        return c
-
-    lax.fori_loop(0, 15, stagey, 0)
-    yc = [remote(yr.at[0], yr.at[2], send, recv, 9, "gy", 1), remote(yr.at[1], yr.at[3], send, recv, 10, "gy", -1)]
     for c in g1:
         c.wait()
     mine = ix * 4 + iy
@@ -467,10 +467,8 @@
     lax.fori_loop(0, (live + FEW - 1) // FEW, body, 0)
 
 
-def residual_stage(E0, G, Ec, Wc, xk, E, R, K, W, gk, C, gc, inner, sem):
+def residual_stage(E, G, Ec, Wc, xk, R, K, W, gk, C, gc, inner):
     lane, sub = lanes_sub()
-    whole = pltpu.make_async_copy(E0, E, sem)
-    whole.start()
     near = (lane < 8) | (lane >= 120)
 
     def unpack(n, c):
@@ -487,7 +485,6 @@
 
     lax.fori_loop(0, 42, unpack, 0)
 
-    whole.wait()
     for f in range(3):
         for k in range(5):
             for d, y0 in ((0, 3), (1, 40)):
@@ -542,8 +539,8 @@
     lax.fori_loop(0, 32, keep, 0)
 
 
-def enrich_kernel(live_ref, off, E0, G, Ec, Wc, xk, out, corr, inner, E, R, K, W, gk, C, gc, cbuf, vbuf, sem):
-    residual_stage(E0, G, Ec, Wc, xk, E, R, K, W, gk, C, gc, inner, sem)
+def enrich_kernel(live_ref, off, E, G, Ec, Wc, xk, out, corr, inner, R, K, W, gk, C, gc, cbuf, vbuf):
+    residual_stage(E, G, Ec, Wc, xk, R, K, W, gk, C, gc, inner)
     live = jnp.clip(live_ref[0], 0, NP)
     corr[...] = jnp.zeros_like(corr)
     lane, sub = lanes_sub()
@@ -670,9 +667,9 @@
 def enrich(live, off, E, G, Ec, Wc, xk):
     return pl.pallas_call(
         enrich_kernel, out_shape=(f32(NP * 64, 128), f32(2, 52, 48, 128), f32(32, 32, 128)),
-        in_specs=[SM, SM, pl.BlockSpec(memory_space=pl.ANY), VM, VM, VM, VM], out_specs=(VM, VM, VM),
-        scratch_shapes=[vmem(3 * 48 * 48, 128), vmem(2, 40, 40, 128), vmem(2, 40, 40, 128), vmem(2, 40, 40, 128),
-                        vmem(56, 48, 128), vmem(56, 48, 128), vmem(56, 48, 128), vmem(PAIR, 192, 128), vmem(PAIR, 64, 128), pltpu.SemaphoreType.DMA],
+        in_specs=[SM, SM, VM, VM, VM, VM, VM], out_specs=(VM, VM, VM),
+        scratch_shapes=[vmem(2, 40, 40, 128), vmem(2, 40, 40, 128), vmem(2, 40, 40, 128),
+                        vmem(56, 48, 128), vmem(56, 48, 128), vmem(56, 48, 128), vmem(PAIR, 192, 128), vmem(PAIR, 64, 128)],
         compiler_params=pltpu.CompilerParams(vmem_limit_bytes=30 << 20), name="enrich")(live, off, E, G, Ec, Wc, xk)
 
 

time: 126 us -> 124 us (0.984)
  the two profiles are of different devices: /device:TPU:10 before, /device:TPU:7 now
where the time goes in v2:
time: 124 us; the launch traced here: 122 us
  Pallas kernels  120 us (97%)
  between operations  1.34 us (1%)
    pallas_call x1, Pallas kernels, fold(): pl.pallas_call(fold_kernel, out_shape=f32(1024, 128), in_specs=[VM, VM],...  34.6 us
    pallas_call x1, Pallas kernels, enrich(): pl.pallas_call(enrich_kernel, out_shape=(f32(NP * 64, 128), f32(2, 52, 48...  30.7 us
    pallas_call x1, Pallas kernels, share(): pl.pallas_call(share_kernel, out_shape=(f32(16, 4, 8, 128), f32(3 * 48 *...  27.4 us
    pallas_call x1, Pallas kernels, merge(): pl.pallas_call(merge_kernel, out_shape=(f32(48, 48, 128), f32(2, 7, 48, 1...  25.5 us

profile of v2, /device:TPU:7, one launch (start us, length us, event | category | flops | bytes accessed | tf_op | source)
XLA Modules:
  0.0 122.4 jit_solution(6018982553294842333)
XLA Ops:
  1.3 0.0 copy-start
  1.3 0.0 copy-start.1
  1.3 27.4 %share.1 = (f32[16,4,8,128]{3,2,1,0:T(8,128)S(1)}, f32[6912,128]{1,0:T(8,128)S(1)}, f32[3,7,48,128]{3,2,1,0:T(8,128)S(1)}, f32[2,2,3,5,8,128]{5,4,3,2,1,0:T(8,128)S(1)}, f32[10240,128]{1,0:T(8,128)S(1)}) custom-call(f32[8,64]{1,0:T(8,128)} %bitcast.34, f32[1024,128]{1,0:T(8,128)} %bitcast.31, f32[1024,128]{1,0:T(8,128)} %bitcast.32, s32[1024,128]{1,0:T(8,128)} %bitcast.33, ...), custom_call_target="tpu_custom_call" | custom-call | tf_op jit(solution)/shard_map/share/pallas_call | solution.py:401
  28.7 0.0 copy-done
  28.7 0.0 copy-done.1
  28.7 2.1 %prolong.1.T = f32[2,52,48,128]{3,2,1,0:T(8,128)S(1)} custom-call(s32[1]{0:T(128)} %bitcast.24.live_ref, s32[3,1,40]{2,1,0:T(1,128)S(1)} %bitcast.27, s32[4,40]{1,0:T(4,128)S(1)} %bitcast.29, f32[16,4,8,128]{3,2,1,0:T(8,128)S(1)} %get-tuple-element.15.gat, f32[10240,128]{1,0:T(8,128)S(1)} %get-tuple-element.16.buf), custom_call_target="tpu_custom_call" | custom-call | tf_op jit(solution)/shard_map/prolong/pallas_call | solution.py:662
  30.8 25.5 %merge.1 = (f32[48,48,128]{2,1,0:T(8,128)S(1)}, f32[2,7,48,128]{3,2,1,0:T(8,128)S(1)}, f32[3,7,48,128]{3,2,1,0:T(8,128)S(1)}, f32[2,2,3,5,8,128]{5,4,3,2,1,0:T(8,128)S(1)}) custom-call(f32[2,52,48,128]{3,2,1,0:T(8,128)S(1)} %prolong.1.T, f32[3,7,48,128]{3,2,1,0:T(8,128)S(1)} %get-tuple-element.17.G0, f32[2,2,3,5,8,128]{5,4,3,2,1,0:T(8,128)S(1)} %get-tuple-element.18.yk), custom_call_target="tpu_custom_call" | custom-call | tf_op jit(solution)/shard_map/merge/pallas_call | solution.py:412
  56.3 30.7 %enrich.1 = (f32[2560,128]{1,0:T(8,128)}, f32[2,52,48,128]{3,2,1,0:T(8,128)S(1)}, f32[32,32,128]{2,1,0:T(8,128)S(1)}) custom-call(s32[1]{0:T(128)} %bitcast.25.live_ref, s32[3,1,40]{2,1,0:T(1,128)S(1)} %bitcast.28, f32[6912,128]{1,0:T(8,128)S(1)} %get-tuple-element.14.E, f32[3,7,48,128]{3,2,1,0:T(8,128)S(1)} %get-tuple-element.19.G, ...), custom_call_target="tpu_custom_call" | custom-call | tf_op jit(solution)/shard_map/enrich/pallas_call | solution.py:668
  87.0 34.6 %fold.1 = f32[1024,128]{1,0:T(8,128)S(1)} custom-call(f32[2,52,48,128]{3,2,1,0:T(8,128)S(1)} %get-tuple-element.23.T, f32[32,32,128]{2,1,0:T(8,128)S(1)} %get-tuple-element.24.C), custom_call_target="tpu_custom_call" | custom-call | tf_op jit(solution)/shard_map/fold/pallas_call | solution.py:423
  121.6 0.8 copy.15
Async XLA Ops:
  1.3 27.4 %copy-start = (s32[1,1,1,40,3]{3,2,4,1,0:T(1,128)S(1)}, s32[1,1,1,40,3]{3,2,4,1,0:T(1,128)}, u32[]{:S(2)}) copy-start(s32[1,1,1,40,3]{3,2,4,1,0:T(1,128)} %param.17) | copy-start | bytes 1444
  1.3 27.4 %copy-start.1 = (s32[1,1,1,40,4]{3,4,2,1,0:T(4,128)S(1)}, s32[1,1,1,40,4]{3,4,2,1,0:T(4,128)}, u32[]{:S(2)}) copy-start(s32[1,1,1,40,4]{3,4,2,1,0:T(4,128)} %param.16) | copy-start | bytes 1924
